TPU v7x, 512 devices: a whole 4x4x16 slice. The times are simulated.
512 devices in a mesh: rep: 2 (over core), row: 16 (over y, x), col: 16 (over z).
Axes of the slice: x: 4, y: 4, z: 16, core: 2. Of those that a mesh axis runs over, the one named last changes fastest.
Arguments:
- residual: bfloat16 [16384, 2048], P(('rep', 'row'), 'col'), may hold values from -6 to 6
- post_gain: float32 [2048], replicated, may hold values from 0.25 to 1.75
- w_gate: bfloat16 [2048, 6144], P('row', 'col'), may hold values from -0.125 to 0.125
- w_up: bfloat16 [2048, 6144], P('row', 'col'), may hold values from -0.125 to 0.125
- w_down: bfloat16 [6144, 2048], P('col', 'row'), may hold values from -0.078125 to 0.078125
- next_gain: float32 [2048], replicated, may hold values from 0.25 to 1.75
- w_qkv: bfloat16 [2048, 4096], P('row', 'col'), may hold values from -0.125 to 0.125
- q_gain: float32 [128], replicated, may hold values from 0.25 to 1.75
- k_gain: float32 [128], replicated, may hold values from 0.25 to 1.75
- source: int32 [16384], P(('rep', 'row')), may hold values from 0 to 16383, as said below
Outputs:
- moved_residual: bfloat16 [16384, 2048], P(('rep', 'row'), 'col')
- moved_qkv: bfloat16 [16384, 4096], P(('rep', 'row'), 'col')
Inputs may be any that keep to these rules, and one draw needn't show every extreme that they name: source is a permutation of all rows. Rows are grouped in blocks of 512 (block b holds rows b * 512 to (b + 1) * 512 - 1, blocks of replica 0 first); output block b takes its rows from input block b or from the block of the same row index in the other replica, at most 128 of them from the other replica, and some block takes exactly 128. A block takes as many rows from the other replica as it gives to it.
All inputs are finite; a program needn't handle non-finite values.
Results may differ from a plain program's by a relative error of at most 0.0065.
Values may be sent and summed in bfloat16 or wider, within the bound.
A program may use at most 64 MiB of HBM per device.

v0:
```python
import jax
import jax.numpy as jnp
from jax import lax
from jax.sharding import PartitionSpec as P

HEADS = 16
KV_HEADS = 8
HD = 128
epsilon = 1e-06


def swapped(x, axis, apart):
    return lax.ppermute(x, axis, [(i, i ^ 1 << apart) for i in range(lax.axis_size(axis))])


def normalize(values, gain):
    scale = lax.rsqrt(jnp.mean(values * values, axis=-1, keepdims=True) + epsilon)
    return values * scale * gain


def per_device(residual, post_gain, w_gate, w_up, w_down, next_gain, w_qkv, q_gain, k_gain, source):
    tok_rows = residual.shape[0]
    col_index = lax.axis_index("col")
    gathered = lax.all_gather(residual, "col", axis=1, tiled=True)
    stream = gathered.astype(jnp.float32)
    normed = normalize(stream, post_gain).astype(jnp.bfloat16)
    columns = normed
    gate_proj = jnp.dot(
        columns,
        lax.all_gather(w_gate, "row", axis=0, tiled=True),
        preferred_element_type=jnp.float32,
    )
    up_proj = jnp.dot(
        columns, lax.all_gather(w_up, "row", axis=0, tiled=True), preferred_element_type=jnp.float32
    )
    hidden = (jax.nn.silu(gate_proj) * up_proj).astype(jnp.bfloat16)
    partial_value = jnp.dot(
        hidden,
        lax.all_gather(w_down, "row", axis=1, tiled=True),
        preferred_element_type=jnp.float32,
    )
    mlp_share = lax.psum_scatter(partial_value, "col", scatter_dimension=1, tiled=True)
    resid_own = (residual.astype(jnp.float32) + mlp_share).astype(jnp.bfloat16)
    resid_full = lax.all_gather(resid_own, "col", axis=1, tiled=True)
    next_normed = normalize(resid_full.astype(jnp.float32), next_gain).astype(jnp.bfloat16)
    proj_width = w_qkv.shape[1]
    columns = next_normed
    projected = jnp.dot(
        columns,
        lax.all_gather(w_qkv, "row", axis=0, tiled=True),
        preferred_element_type=jnp.float32,
    )
    head_count = proj_width // HD
    per_head = projected.reshape(tok_rows, head_count, HD)
    head_number = col_index * head_count + jnp.arange(head_count, dtype=jnp.int32)
    is_query = head_number < HEADS
    is_key = jnp.logical_and(head_number >= HEADS, head_number < HEADS + KV_HEADS)
    head_gain = jnp.where(is_query[:, None], q_gain[None, :], k_gain[None, :])
    head_scaled = normalize(per_head, head_gain)
    keep_norm = jnp.logical_or(is_query, is_key)[None, :, None]
    qkv_own = (
        jnp.where(keep_norm, head_scaled, per_head)
        .reshape(tok_rows, proj_width)
        .astype(jnp.bfloat16)
    )
    my_block = lax.axis_index("rep") * lax.axis_size("row") + lax.axis_index("row")
    from_peer = source // tok_rows != my_block
    local_row = source % tok_rows
    peer_resid, peer_qkv = swapped((resid_own, qkv_own), "rep", 0)
    picked = local_row + tok_rows * from_peer.astype(jnp.int32)
    moved_residual = jnp.take(jnp.concatenate([resid_own, peer_resid], axis=0), picked, axis=0)
    moved_qkv = jnp.take(jnp.concatenate([qkv_own, peer_qkv], axis=0), picked, axis=0)
    return (moved_residual, moved_qkv)


def solution(mesh):
    return jax.shard_map(
        per_device,
        mesh=mesh,
        in_specs=(
            P(("rep", "row"), "col"),
            P(),
            P("row", "col"),
            P("row", "col"),
            P("col", "row"),
            P(),
            P("row", "col"),
            P(),
            P(),
            P(("rep", "row")),
        ),
        out_specs=(P(("rep", "row"), "col"), P(("rep", "row"), "col")),
        check_vma=False,
    )
```

profile of v0, /device:TPU:1, one launch (start us, length us, event | category | flops | bytes accessed | tf_op | source)
XLA Modules:
  0.0 517.1 jit_solution(11629037548047053310)
XLA Ops:
  7.2 0.7 all-gather.7.cloned.1.call-update
  8.0 0.7 all-gather.9.cloned.1.call-update
  8.7 0.7 all-gather.11.cloned.1.call-update
  9.4 0.5 all-gather.13.cloned.1.call-update
  10.0 74.2 %all-gather.7.cloned.1.call-done = bf16[512,2048]{1,0:T(8,128)(2,1)} async-done(((bf16[512,128]{1,0:T(8,128)(2,1)}), bf16[512,2048]{1,0:T(8,128)(2,1)}) %all-gather.7.cloned.1.call-update) | async-done | bytes 2097168 | tf_op jit(solution)/shard_map/all_gather | solution.py:24
  84.2 2.2 fusion
  86.4 65.4 %all-gather.9.cloned.1.call-done = bf16[2048,384]{1,0:T(8,128)(2,1)} async-done(((bf16[128,384]{1,0:T(8,128)(2,1)}), bf16[2048,384]{1,0:T(8,128)(2,1)}) %all-gather.9.cloned.1.call-update) | async-done | bytes 1572880 | tf_op jit(solution)/shard_map/all_gather | solution.py:30
  151.8 2.7 fusion.19
  154.5 59.1 %all-gather.11.cloned.1.call-done = bf16[2048,384]{1,0:T(8,128)(2,1)} async-done(((bf16[128,384]{1,0:T(8,128)(2,1)}), bf16[2048,384]{1,0:T(8,128)(2,1)}) %all-gather.11.cloned.1.call-update) | async-done | bytes 1572880 | tf_op jit(solution)/shard_map/all_gather | solution.py:34
  213.6 62.7 %all-gather.13.cloned.1.call-done = bf16[384,2048]{1,0:T(8,128)(2,1)} async-done(((bf16[384,128]{1,0:T(8,128)(2,1)}), bf16[384,2048]{1,0:T(8,128)(2,1)}) %all-gather.13.cloned.1.call-update) | async-done | bytes 1572880 | tf_op jit(solution)/shard_map/all_gather | solution.py:39
  276.3 6.2 %fusion.11 = f32[512,2048]{1,0:T(8,128)} fusion(bf16[384,2048]{1,0:T(8,128)(2,1)} %all-gather.13.cloned.1.call-done, bf16[2048,384]{1,0:T(8,128)(2,1)} %all-gather.11.cloned.1.call-done, f32[512,384]{1,0:T(8,128)S(1)} %fusion.19, bf16[512,2048]{1,0:T(8,128)(2,1)S(1)} %copy-done.1, f32[2048]{0:T(1024)S(1)} %copy-done.7, f32[512]{0:T(512)S(1)} %add_rsqrt_fusion.2), kind=kOutput, calls=%fused_computation.17 | convolution fusion | flops 1615986688 | bytes 10233856 | tf_op jit(solution)/shard_map/dot_general | solution.py:37
  282.6 71.0 %reduce-scatter.2.cloned.1.call-done = f32[512,128]{1,0:T(8,128)} async-done(((f32[512,2048]{1,0:T(8,128)}), f32[512,128]{1,0:T(8,128)}) %reduce-scatter.2.cloned.1.call-update) | async-done | bytes 262160 | tf_op jit(solution)/shard_map/reduce_scatter | solution.py:42
  353.6 1.6 add_convert_fusion
  355.3 0.7 all-gather.17.cloned.1.call-update
  356.3 11.9 %collective-permute-start = (bf16[512,128]{1,0:T(8,128)(2,1)}, bf16[512,128]{1,0:T(8,128)(2,1)S(1)}, u32[]{:S(2)}, u32[]{:S(2)}) collective-permute-start(bf16[512,128]{1,0:T(8,128)(2,1)} %add_convert_fusion), channel_id=1, source_target_pairs={{0,256},{256,0},{1,257},{257,1},{2,258},{258,2},{3,259},{259,3},{4... | collective-permute-start | bytes 393224 | tf_op jit(solution)/shard_map/ppermute | solution.py:13
  368.2 64.5 %all-gather.15.cloned.1.call-done = bf16[512,2048]{1,0:T(8,128)(2,1)} async-done(((bf16[512,128]{1,0:T(8,128)(2,1)}), bf16[512,2048]{1,0:T(8,128)(2,1)}) %all-gather.15.cloned.1.call-update) | async-done | bytes 2097168 | tf_op jit(solution)/shard_map/all_gather | solution.py:44
  432.6 2.2 fusion.3
  434.9 63.7 %all-gather.17.cloned.1.call-done = bf16[2048,256]{1,0:T(8,128)(2,1)} async-done(((bf16[128,256]{1,0:T(8,128)(2,1)}), bf16[2048,256]{1,0:T(8,128)(2,1)}) %all-gather.17.cloned.1.call-update) | async-done | bytes 1048592 | tf_op jit(solution)/shard_map/all_gather | solution.py:50
  498.6 2.2 bitcast_reduce_fusion
  500.9 4.0 collective-permute-start.1
  505.0 1.3 gather_fusion
  506.3 0.8 broadcast_select_fusion.1
  507.4 2.0 gather_fusion.1
  509.4 0.8 broadcast_select_fusion
  (41 shorter events, 1.0 us)
Async XLA Ops:
  7.2 144.7 %copy-start.7 = (f32[2048]{0:T(1024)S(1)}, f32[2048]{0:T(1024)}, u32[]{:S(2)}) copy-start(f32[2048]{0:T(1024)} %param.11) | copy-start | bytes 24580
  7.2 77.0 %all-gather.7.cloned.1.call-start = ((), (), s32[]{:S(2)}) async-start(), calls=%async_computation.1 | async-start | bytes 2228224 | tf_op jit(solution)/shard_map/all_gather | solution.py:24
  7.9 143.9 %all-gather.9.cloned.1.call-start = ((), (), s32[]{:S(2)}) async-start(), calls=%async_computation.2 | async-start | bytes 1671168 | tf_op jit(solution)/shard_map/all_gather | solution.py:30
  8.7 204.9 %all-gather.11.cloned.1.call-start = ((), (), s32[]{:S(2)}) async-start(), calls=%async_computation.3 | async-start | bytes 1671168 | tf_op jit(solution)/shard_map/all_gather | solution.py:34
  9.4 266.9 %all-gather.13.cloned.1.call-start = ((), (), s32[]{:S(2)}) async-start(), calls=%async_computation.4 | async-start | bytes 1671168 | tf_op jit(solution)/shard_map/all_gather | solution.py:39
  10.0 343.7 %reduce-scatter.2.cloned.1.call-start = ((), (), s32[]{:S(2)}) async-start(), calls=%async_computation.5 | async-start | bytes 4456448 | tf_op jit(solution)/shard_map/reduce_scatter | solution.py:42
  84.2 67.6 %copy-start.1 = (bf16[512,2048]{1,0:T(8,128)(2,1)S(1)}, bf16[512,2048]{1,0:T(8,128)(2,1)}, u32[]{:S(2)}) copy-start(bf16[512,2048]{1,0:T(8,128)(2,1)} %all-gather.7.cloned.1.call-done) | copy-start | bytes 6291460
  282.5 71.1 %copy-start.3 = (bf16[512,128]{1,0:T(8,128)(2,1)S(1)}, bf16[512,128]{1,0:T(8,128)(2,1)}, u32[]{:S(2)}) copy-start(bf16[512,128]{1,0:T(8,128)(2,1)} %param.10) | copy-start | bytes 393220
  282.6 73.5 %copy-start.4 = (s32[512]{0:T(512)S(1)}, s32[512]{0:T(512)}, u32[]{:S(2)}) copy-start(s32[512]{0:T(512)} %param.19) | copy-start | bytes 6148
  282.6 73.6 %copy-start.5 = (f32[128]{0:T(128)S(1)}, f32[128]{0:T(128)}, u32[]{:S(2)}) copy-start(f32[128]{0:T(128)} %param.18) | copy-start | bytes 1540
  282.6 73.6 %copy-start.6 = (f32[128]{0:T(128)S(1)}, f32[128]{0:T(128)}, u32[]{:S(2)}) copy-start(f32[128]{0:T(128)} %param.17) | copy-start | bytes 1540
  282.6 216.0 %copy-start.8 = (f32[2048]{0:T(1024)S(1)}, f32[2048]{0:T(1024)}, u32[]{:S(2)}) copy-start(f32[2048]{0:T(1024)} %param.15) | copy-start | bytes 24580
  282.6 150.0 %all-gather.15.cloned.1.call-start = ((), (), s32[]{:S(2)}) async-start(), calls=%async_computation.6 | async-start | bytes 2228224 | tf_op jit(solution)/shard_map/all_gather | solution.py:44
  355.3 143.3 %all-gather.17.cloned.1.call-start = ((), (), s32[]{:S(2)}) async-start(), calls=%async_computation.7 | async-start | bytes 1114112 | tf_op jit(solution)/shard_map/all_gather | solution.py:50
  356.3 148.7 %collective-permute-start = (bf16[512,128]{1,0:T(8,128)(2,1)}, bf16[512,128]{1,0:T(8,128)(2,1)S(1)}, u32[]{:S(2)}, u32[]{:S(2)}) collective-permute-start(bf16[512,128]{1,0:T(8,128)(2,1)} %add_convert_fusion), channel_id=1, source_target_pairs={{0,256},{256,0},{1,257},{257,1},{2,258},{258,2},{3,259},{259,3},{4... | collective-permute-start | bytes 393224 | tf_op jit(solution)/shard_map/ppermute | solution.py:13
  432.6 65.9 %copy-start = (bf16[512,2048]{1,0:T(8,128)(2,1)S(1)}, bf16[512,2048]{1,0:T(8,128)(2,1)}, u32[]{:S(2)}) copy-start(bf16[512,2048]{1,0:T(8,128)(2,1)} %all-gather.15.cloned.1.call-done) | copy-start | bytes 6291460
  434.9 70.1 %copy-start.2 = (bf16[512,128]{1,0:T(8,128)(2,1)S(1)}, bf16[512,128]{1,0:T(8,128)(2,1)}, u32[]{:S(2)}) copy-start(bf16[512,128]{1,0:T(8,128)(2,1)} %add_convert_fusion) | copy-start | bytes 393220
  500.9 6.2 %collective-permute-start.1 = (bf16[512,256]{0,1:T(8,128)(2,1)S(1)}, bf16[512,256]{0,1:T(8,128)(2,1)S(1)}, u32[]{:S(2)}, u32[]{:S(2)}) collective-permute-start(bf16[512,256]{0,1:T(8,128)(2,1)S(1)} %fusion.23), channel_id=1, source_target_pairs={{0,256},{256,0},{1,257},{257,1},{2,258},{258,2},{3,259},{259,3},{4... | collective-permute-start | bytes 786440 | tf_op jit(solution)/shard_map/ppermute | solution.py:13
Sparse Core Ops, SparseCore 0:
  10.0 74.1 all-gather.6
  87.2 64.5 all-gather.8
  154.8 58.7 all-gather.10
  216.4 59.8 all-gather.12
  282.7 70.8 reduce-scatter.1
  356.1 76.5 all-gather.14
  435.7 62.8 all-gather.16
where the time goes:
time: 517 us
  waiting for transfers between devices  464 us (90%)
  starting transfers between devices  16.2 us (3%)
  between operations  14.3 us (3%)
  matrix products  11.1 us (2%)
  other arithmetic  8.07 us (2%)
    all_gather x1, waiting for transfers between devices, per_device(): gathered = lax.all_gather(residual, 'col', axis=1, tiled=True)  74.2 us
    reduce_scatter x1, waiting for transfers between devices, per_device(): lax.psum_scatter(partial_value, 'col', scatter_dimension=1, tiled=True)  71 us
    all_gather x1, waiting for transfers between devices, per_device(): lax.all_gather(w_gate, 'row', axis=0, tiled=True)  65.4 us
    all_gather x1, waiting for transfers between devices, per_device(): resid_full = lax.all_gather(resid_own, 'col', axis=1, tiled=True)  64.5 us
    all_gather x1, waiting for transfers between devices, per_device(): lax.all_gather(w_qkv, 'row', axis=0, tiled=True)  63.7 us
    all_gather x1, waiting for transfers between devices, per_device(): lax.all_gather(w_down, 'row', axis=1, tiled=True)  62.7 us
    all_gather x1, waiting for transfers between devices, per_device(): lax.all_gather(w_up, 'row', axis=0, tiled=True)  59.1 us
    ppermute x2, starting transfers between devices, swapped(): lax.ppermute(x, axis, [(i, i ^ 1 << apart) for i in range(lax.axis_size(a...  15.9 us
  transfers between devices with their start and end apart: 9, of which 7 were waited for; matrix products, arithmetic and copies ran while one was open for 2% of the time, Pallas kernels for 0%

commit v1 on v0

--- a/solution.py
+++ b/solution.py
@@ -7,6 +7,19 @@
 KV_HEADS = 8
 HD = 128
 epsilon = 1e-06
+
+
+def ring_gather(x, axis, dim):
+    ways = lax.axis_size(axis)
+    up = [(d, (d + 1) % ways) for d in range(ways)]
+    down = [(d, (d - 1) % ways) for d in range(ways)]
+    earlier, later = ([x], [x])
+    for _ in range(ways // 2):
+        earlier.append(lax.ppermute(earlier[-1], axis, up))
+    for _ in range((ways - 1) // 2):
+        later.append(lax.ppermute(later[-1], axis, down))
+    line = jnp.concatenate([*earlier[::-1], *later[1:]], axis=dim)
+    return jnp.roll(line, (lax.axis_index(axis) - ways // 2) * x.shape[dim], axis=dim)
 
 
 def swapped(x, axis, apart):
@@ -35,9 +48,7 @@
     )
     hidden = (jax.nn.silu(gate_proj) * up_proj).astype(jnp.bfloat16)
     partial_value = jnp.dot(
-        hidden,
-        lax.all_gather(w_down, "row", axis=1, tiled=True),
-        preferred_element_type=jnp.float32,
+        hidden, ring_gather(w_down, "row", 1), preferred_element_type=jnp.float32
     )
     mlp_share = lax.psum_scatter(partial_value, "col", scatter_dimension=1, tiled=True)
     resid_own = (residual.astype(jnp.float32) + mlp_share).astype(jnp.bfloat16)

time: 517 us -> 455 us (0.88)
  waiting for transfers between devices: 464 us -> 312 us
  starting transfers between devices: 16.2 us -> 81.3 us
  local copies, waits for them, and re-layouts: 3.61 us -> 25.9 us
    all_gather x1, waiting for transfers between devices: 74.2 us -> 0.01 us  [per_device(): gathered = lax.all_gather(residual, 'col', axis=1, tiled=True)]
    ppermute x0 -> x15, starting transfers between devices: none -> 64.8 us  [the longest x7 47.5 us: ring_gather(): later.append(lax.ppermute(later[-1], axis, down))]
    all_gather x1 -> x0, waiting for transfers between devices: 62.7 us -> none  [per_device(): lax.all_gather(w_down, 'row', axis=1, tiled=True)]
    unnamed x18 -> x49, local copies, waits for them, and re-layouts: 0.04 us -> 21.7 us
    all_gather x1, waiting for transfers between devices: 65.4 us -> 45.9 us  [per_device(): lax.all_gather(w_gate, 'row', axis=0, tiled=True)]
    ppermute x0 -> x15, waiting for transfers between devices: none -> 7.2 us  [the longest x8 7.18 us: ring_gather(): earlier.append(lax.ppermute(earlier[-1], axis, up))]
  transfers between devices with their start and end apart: 9 -> 23, of which waited for: 7 -> 11; matrix products, arithmetic and copies ran while one was open for 2% -> 8% of each run, Pallas kernels for 0% -> 0%
where the time goes in v1:
time: 455 us; the launch traced here: 454 us
  waiting for transfers between devices  312 us (69%)
  starting transfers between devices  81.3 us (18%)
  local copies, waits for them, and re-layouts  25.9 us (6%)
  between operations  14.5 us (3%)
  matrix products  12.4 us (3%)
  other arithmetic  7.77 us (2%)
    reduce_scatter x1, waiting for transfers between devices, per_device(): lax.psum_scatter(partial_value, 'col', scatter_dimension=1, tiled=True)  70.7 us
    all_gather x1, waiting for transfers between devices, per_device(): resid_full = lax.all_gather(resid_own, 'col', axis=1, tiled=True)  64.1 us
    all_gather x1, waiting for transfers between devices, per_device(): lax.all_gather(w_qkv, 'row', axis=0, tiled=True)  63.7 us
    all_gather x1, waiting for transfers between devices, per_device(): lax.all_gather(w_up, 'row', axis=0, tiled=True)  58.4 us
    ppermute x7, starting transfers between devices, ring_gather(): later.append(lax.ppermute(later[-1], axis, down))  47.5 us
    all_gather x1, waiting for transfers between devices, per_device(): lax.all_gather(w_gate, 'row', axis=0, tiled=True)  45.9 us
    unnamed x49, local copies, waits for them, and re-layouts  21.7 us
    ppermute x8, starting transfers between devices, ring_gather(): earlier.append(lax.ppermute(earlier[-1], axis, up))  17.3 us
  transfers between devices with their start and end apart: 23, of which 11 were waited for; matrix products, arithmetic and copies ran while one was open for 8% of the time, Pallas kernels for 0%

profile of v1, /device:TPU:1, one launch (start us, length us, event | category | flops | bytes accessed | tf_op | source)
XLA Modules:
  0.0 453.8 jit_solution(6958949865879156038)
XLA Ops:
  8.7 4.0 collective-permute-start
  12.7 5.9 %collective-permute-done = bf16[384,128]{1,0:T(8,128)(2,1)S(1)} collective-permute-done((bf16[384,128]{1,0:T(8,128)(2,1)}, bf16[384,128]{1,0:T(8,128)(2,1)S(1)}, u32[]{:S(2)}, u32[]{:S(2)}) %collective-permute-start) | collective-permute-done | bytes 98336 | tf_op jit(solution)/shard_map/ppermute | solution.py:18
  20.5 6.7 %collective-permute-start.8 = (bf16[384,128]{1,0:T(8,128)(2,1)}, bf16[384,128]{1,0:T(8,128)(2,1)S(1)}, u32[]{:S(2)}, u32[]{:S(2)}) collective-permute-start(bf16[384,128]{1,0:T(8,128)(2,1)} %param.14), channel_id=1, source_target_pairs={{0,240},{16,0},{32,16},{48,32},{64,48},{80,64},{96,80},{112,96},{1... | collective-permute-start | bytes 294920 | tf_op jit(solution)/shard_map/ppermute | solution.py:20
  29.2 6.9 %collective-permute-start.9 = (bf16[384,128]{1,0:T(8,128)(2,1)S(1)}, bf16[384,128]{1,0:T(8,128)(2,1)S(1)}, u32[]{:S(2)}, u32[]{:S(2)}) collective-permute-start(bf16[384,128]{1,0:T(8,128)(2,1)S(1)} %collective-permute-done.8), channel_id=1, source_target_pairs={{0,240},{16,0},{32,16},{48,32},{64,48},{80,64},{96,80},{112,96},{1... | collective-permute-start | bytes 294920 | tf_op jit(solution)/shard_map/ppermute | solution.py:20
  36.1 1.9 collective-permute-start.3
  38.0 6.9 %collective-permute-start.10 = (bf16[384,128]{1,0:T(8,128)(2,1)S(1)}, bf16[384,128]{1,0:T(8,128)(2,1)S(1)}, u32[]{:S(2)}, u32[]{:S(2)}) collective-permute-start(bf16[384,128]{1,0:T(8,128)(2,1)S(1)} %collective-permute-done.9), channel_id=1, source_target_pairs={{0,240},{16,0},{32,16},{48,32},{64,48},{80,64},{96,80},{112,96},{1... | collective-permute-start | bytes 294920 | tf_op jit(solution)/shard_map/ppermute | solution.py:20
  47.7 7.0 %collective-permute-start.11 = (bf16[384,128]{1,0:T(8,128)(2,1)S(1)}, bf16[384,128]{1,0:T(8,128)(2,1)S(1)}, u32[]{:S(2)}, u32[]{:S(2)}) collective-permute-start(bf16[384,128]{1,0:T(8,128)(2,1)S(1)} %collective-permute-done.10), channel_id=1, source_target_pairs={{0,240},{16,0},{32,16},{48,32},{64,48},{80,64},{96,80},{112,96},{1... | collective-permute-start | bytes 294920 | tf_op jit(solution)/shard_map/ppermute | solution.py:20
  54.9 1.9 collective-permute-start.5
  56.8 6.7 %collective-permute-start.12 = (bf16[384,128]{1,0:T(8,128)(2,1)S(1)}, bf16[384,128]{1,0:T(8,128)(2,1)S(1)}, u32[]{:S(2)}, u32[]{:S(2)}) collective-permute-start(bf16[384,128]{1,0:T(8,128)(2,1)S(1)} %collective-permute-done.11), channel_id=1, source_target_pairs={{0,240},{16,0},{32,16},{48,32},{64,48},{80,64},{96,80},{112,96},{1... | collective-permute-start | bytes 294920 | tf_op jit(solution)/shard_map/ppermute | solution.py:20
  65.5 6.7 %collective-permute-start.13 = (bf16[384,128]{1,0:T(8,128)(2,1)S(1)}, bf16[384,128]{1,0:T(8,128)(2,1)S(1)}, u32[]{:S(2)}, u32[]{:S(2)}) collective-permute-start(bf16[384,128]{1,0:T(8,128)(2,1)S(1)} %collective-permute-done.12), channel_id=1, source_target_pairs={{0,240},{16,0},{32,16},{48,32},{64,48},{80,64},{96,80},{112,96},{1... | collective-permute-start | bytes 294920 | tf_op jit(solution)/shard_map/ppermute | solution.py:20
  74.3 6.7 %collective-permute-start.14 = (bf16[384,128]{1,0:T(8,128)(2,1)S(1)}, bf16[384,128]{1,0:T(8,128)(2,1)S(1)}, u32[]{:S(2)}, u32[]{:S(2)}) collective-permute-start(bf16[384,128]{1,0:T(8,128)(2,1)S(1)} %collective-permute-done.13), channel_id=1, source_target_pairs={{0,240},{16,0},{32,16},{48,32},{64,48},{80,64},{96,80},{112,96},{1... | collective-permute-start | bytes 294920 | tf_op jit(solution)/shard_map/ppermute | solution.py:20
  103.3 2.1 fusion
  105.4 45.9 %all-gather.8.cloned.1.call-done = bf16[2048,384]{1,0:T(8,128)(2,1)} async-done(((bf16[128,384]{1,0:T(8,128)(2,1)}), bf16[2048,384]{1,0:T(8,128)(2,1)}) %all-gather.8.cloned.1.call-update) | async-done | bytes 1572880 | tf_op jit(solution)/shard_map/all_gather | solution.py:43
  151.3 3.3 fusion.20
  154.6 58.4 %all-gather.10.cloned.1.call-done = bf16[2048,384]{1,0:T(8,128)(2,1)} async-done(((bf16[128,384]{1,0:T(8,128)(2,1)}), bf16[2048,384]{1,0:T(8,128)(2,1)}) %all-gather.10.cloned.1.call-update) | async-done | bytes 1572880 | tf_op jit(solution)/shard_map/all_gather | solution.py:47
  213.1 6.3 %fusion.10 = f32[512,2048]{1,0:T(8,128)} fusion(bf16[384,4096]{1,0:T(8,128)(2,1)} %constant_dynamic-update-slice_fusion, s32[]{:T(128)S(6)} %select_n.55, bf16[2048,384]{1,0:T(8,128)(2,1)} %all-gather.10.cloned.1.call-done, f32[512,384]{1,0:T(8,128)S(1)} %fusion.20, bf16[512,2048]{1,0:T(8,128)(2,1)S(1)} %copy-done, f32[2048]{0:T(1024)S(1)} %copy-done.7, ...), kind=kOutput, calls=%fused_computation.15 | convolution fusion | flops 1615986688 | bytes 10233860 | tf_op jit(solution)/shard_map/dot_general | solution.py:50
  219.4 70.7 %reduce-scatter.2.cloned.1.call-done = f32[512,128]{1,0:T(8,128)} async-done(((f32[512,2048]{1,0:T(8,128)}), f32[512,128]{1,0:T(8,128)}) %reduce-scatter.2.cloned.1.call-update) | async-done | bytes 262160 | tf_op jit(solution)/shard_map/reduce_scatter | solution.py:53
  292.6 12.2 %collective-permute-start.15 = (bf16[512,128]{1,0:T(8,128)(2,1)}, bf16[512,128]{1,0:T(8,128)(2,1)S(1)}, u32[]{:S(2)}, u32[]{:S(2)}) collective-permute-start(bf16[512,128]{1,0:T(8,128)(2,1)} %add_convert_fusion), channel_id=1, source_target_pairs={{0,256},{256,0},{1,257},{257,1},{2,258},{258,2},{3,259},{259,3},{4... | collective-permute-start | bytes 393224 | tf_op jit(solution)/shard_map/ppermute | solution.py:26
  304.8 64.1 %all-gather.12.cloned.1.call-done = bf16[512,2048]{1,0:T(8,128)(2,1)} async-done(((bf16[512,128]{1,0:T(8,128)(2,1)}), bf16[512,2048]{1,0:T(8,128)(2,1)}) %all-gather.12.cloned.1.call-update) | async-done | bytes 2097168 | tf_op jit(solution)/shard_map/all_gather | solution.py:55
  368.9 2.1 fusion.3
  371.0 63.7 %all-gather.14.cloned.1.call-done = bf16[2048,256]{1,0:T(8,128)(2,1)} async-done(((bf16[128,256]{1,0:T(8,128)(2,1)}), bf16[2048,256]{1,0:T(8,128)(2,1)}) %all-gather.14.cloned.1.call-update) | async-done | bytes 1048592 | tf_op jit(solution)/shard_map/all_gather | solution.py:61
  434.7 2.8 bitcast_reduce_fusion
  437.6 4.0 collective-permute-start.16
  444.1 2.0 gather_fusion.1
  (100 shorter events, 40.6 us)
Async XLA Ops:
  7.2 96.1 %all-gather.6.cloned.1.call-start = ((), (), s32[]{:S(2)}) async-start(), calls=%async_computation.1 | async-start | bytes 2228224 | tf_op jit(solution)/shard_map/all_gather | solution.py:37
  7.9 143.4 %all-gather.8.cloned.1.call-start = ((), (), s32[]{:S(2)}) async-start(), calls=%async_computation.2 | async-start | bytes 1671168 | tf_op jit(solution)/shard_map/all_gather | solution.py:43
  8.7 204.4 %all-gather.10.cloned.1.call-start = ((), (), s32[]{:S(2)}) async-start(), calls=%async_computation.3 | async-start | bytes 1671168 | tf_op jit(solution)/shard_map/all_gather | solution.py:47
  8.7 9.9 %collective-permute-start = (bf16[384,128]{1,0:T(8,128)(2,1)}, bf16[384,128]{1,0:T(8,128)(2,1)S(1)}, u32[]{:S(2)}, u32[]{:S(2)}) collective-permute-start(bf16[384,128]{1,0:T(8,128)(2,1)} %param.14), channel_id=1, source_target_pairs={{0,16},{16,32},{32,48},{48,64},{64,80},{80,96},{96,112},{112,128},... | collective-permute-start | bytes 294920 | tf_op jit(solution)/shard_map/ppermute | solution.py:18
  18.6 8.7 %collective-permute-start.1 = (bf16[384,128]{1,0:T(8,128)(2,1)S(1)}, bf16[384,128]{1,0:T(8,128)(2,1)S(1)}, u32[]{:S(2)}, u32[]{:S(2)}) collective-permute-start(bf16[384,128]{1,0:T(8,128)(2,1)S(1)} %collective-permute-done), channel_id=1, source_target_pairs={{0,16},{16,32},{32,48},{48,64},{64,80},{80,96},{96,112},{112,128},... | collective-permute-start | bytes 294920 | tf_op jit(solution)/shard_map/ppermute | solution.py:18
  20.5 8.7 %collective-permute-start.8 = (bf16[384,128]{1,0:T(8,128)(2,1)}, bf16[384,128]{1,0:T(8,128)(2,1)S(1)}, u32[]{:S(2)}, u32[]{:S(2)}) collective-permute-start(bf16[384,128]{1,0:T(8,128)(2,1)} %param.14), channel_id=1, source_target_pairs={{0,240},{16,0},{32,16},{48,32},{64,48},{80,64},{96,80},{112,96},{1... | collective-permute-start | bytes 294920 | tf_op jit(solution)/shard_map/ppermute | solution.py:20
  27.3 8.8 %collective-permute-start.2 = (bf16[384,128]{1,0:T(8,128)(2,1)S(1)}, bf16[384,128]{1,0:T(8,128)(2,1)S(1)}, u32[]{:S(2)}, u32[]{:S(2)}) collective-permute-start(bf16[384,128]{1,0:T(8,128)(2,1)S(1)} %collective-permute-done.1), channel_id=1, source_target_pairs={{0,16},{16,32},{32,48},{48,64},{64,80},{80,96},{96,112},{112,128},... | collective-permute-start | bytes 294920 | tf_op jit(solution)/shard_map/ppermute | solution.py:18
  29.2 8.8 %collective-permute-start.9 = (bf16[384,128]{1,0:T(8,128)(2,1)S(1)}, bf16[384,128]{1,0:T(8,128)(2,1)S(1)}, u32[]{:S(2)}, u32[]{:S(2)}) collective-permute-start(bf16[384,128]{1,0:T(8,128)(2,1)S(1)} %collective-permute-done.8), channel_id=1, source_target_pairs={{0,240},{16,0},{32,16},{48,32},{64,48},{80,64},{96,80},{112,96},{1... | collective-permute-start | bytes 294920 | tf_op jit(solution)/shard_map/ppermute | solution.py:20
  36.1 9.6 %collective-permute-start.3 = (bf16[384,128]{1,0:T(8,128)(2,1)S(1)}, bf16[384,128]{1,0:T(8,128)(2,1)S(1)}, u32[]{:S(2)}, u32[]{:S(2)}) collective-permute-start(bf16[384,128]{1,0:T(8,128)(2,1)S(1)} %collective-permute-done.2), channel_id=1, source_target_pairs={{0,16},{16,32},{32,48},{48,64},{64,80},{80,96},{96,112},{112,128},... | collective-permute-start | bytes 294920 | tf_op jit(solution)/shard_map/ppermute | solution.py:18
  38.0 9.6 %collective-permute-start.10 = (bf16[384,128]{1,0:T(8,128)(2,1)S(1)}, bf16[384,128]{1,0:T(8,128)(2,1)S(1)}, u32[]{:S(2)}, u32[]{:S(2)}) collective-permute-start(bf16[384,128]{1,0:T(8,128)(2,1)S(1)} %collective-permute-done.9), channel_id=1, source_target_pairs={{0,240},{16,0},{32,16},{48,32},{64,48},{80,64},{96,80},{112,96},{1... | collective-permute-start | bytes 294920 | tf_op jit(solution)/shard_map/ppermute | solution.py:20
  45.7 9.2 %collective-permute-start.4 = (bf16[384,128]{1,0:T(8,128)(2,1)S(1)}, bf16[384,128]{1,0:T(8,128)(2,1)S(1)}, u32[]{:S(2)}, u32[]{:S(2)}) collective-permute-start(bf16[384,128]{1,0:T(8,128)(2,1)S(1)} %collective-permute-done.3), channel_id=1, source_target_pairs={{0,16},{16,32},{32,48},{48,64},{64,80},{80,96},{96,112},{112,128},... | collective-permute-start | bytes 294920 | tf_op jit(solution)/shard_map/ppermute | solution.py:18
  47.7 9.2 %collective-permute-start.11 = (bf16[384,128]{1,0:T(8,128)(2,1)S(1)}, bf16[384,128]{1,0:T(8,128)(2,1)S(1)}, u32[]{:S(2)}, u32[]{:S(2)}) collective-permute-start(bf16[384,128]{1,0:T(8,128)(2,1)S(1)} %collective-permute-done.10), channel_id=1, source_target_pairs={{0,240},{16,0},{32,16},{48,32},{64,48},{80,64},{96,80},{112,96},{1... | collective-permute-start | bytes 294920 | tf_op jit(solution)/shard_map/ppermute | solution.py:20
  54.9 8.7 %collective-permute-start.5 = (bf16[384,128]{1,0:T(8,128)(2,1)S(1)}, bf16[384,128]{1,0:T(8,128)(2,1)S(1)}, u32[]{:S(2)}, u32[]{:S(2)}) collective-permute-start(bf16[384,128]{1,0:T(8,128)(2,1)S(1)} %collective-permute-done.4), channel_id=1, source_target_pairs={{0,16},{16,32},{32,48},{48,64},{64,80},{80,96},{96,112},{112,128},... | collective-permute-start | bytes 294920 | tf_op jit(solution)/shard_map/ppermute | solution.py:18
  56.8 8.7 %collective-permute-start.12 = (bf16[384,128]{1,0:T(8,128)(2,1)S(1)}, bf16[384,128]{1,0:T(8,128)(2,1)S(1)}, u32[]{:S(2)}, u32[]{:S(2)}) collective-permute-start(bf16[384,128]{1,0:T(8,128)(2,1)S(1)} %collective-permute-done.11), channel_id=1, source_target_pairs={{0,240},{16,0},{32,16},{48,32},{64,48},{80,64},{96,80},{112,96},{1... | collective-permute-start | bytes 294920 | tf_op jit(solution)/shard_map/ppermute | solution.py:20
  63.6 8.7 %collective-permute-start.6 = (bf16[384,128]{1,0:T(8,128)(2,1)S(1)}, bf16[384,128]{1,0:T(8,128)(2,1)S(1)}, u32[]{:S(2)}, u32[]{:S(2)}) collective-permute-start(bf16[384,128]{1,0:T(8,128)(2,1)S(1)} %collective-permute-done.5), channel_id=1, source_target_pairs={{0,16},{16,32},{32,48},{48,64},{64,80},{80,96},{96,112},{112,128},... | collective-permute-start | bytes 294920 | tf_op jit(solution)/shard_map/ppermute | solution.py:18
  65.5 8.8 %collective-permute-start.13 = (bf16[384,128]{1,0:T(8,128)(2,1)S(1)}, bf16[384,128]{1,0:T(8,128)(2,1)S(1)}, u32[]{:S(2)}, u32[]{:S(2)}) collective-permute-start(bf16[384,128]{1,0:T(8,128)(2,1)S(1)} %collective-permute-done.12), channel_id=1, source_target_pairs={{0,240},{16,0},{32,16},{48,32},{64,48},{80,64},{96,80},{112,96},{1... | collective-permute-start | bytes 294920 | tf_op jit(solution)/shard_map/ppermute | solution.py:20
  72.3 8.7 %collective-permute-start.7 = (bf16[384,128]{1,0:T(8,128)(2,1)S(1)}, bf16[384,128]{1,0:T(8,128)(2,1)S(1)}, u32[]{:S(2)}, u32[]{:S(2)}) collective-permute-start(bf16[384,128]{1,0:T(8,128)(2,1)S(1)} %collective-permute-done.6), channel_id=1, source_target_pairs={{0,16},{16,32},{32,48},{48,64},{64,80},{80,96},{96,112},{112,128},... | collective-permute-start | bytes 294920 | tf_op jit(solution)/shard_map/ppermute | solution.py:18
  74.2 215.9 %reduce-scatter.2.cloned.1.call-start = ((), (), s32[]{:S(2)}) async-start(), calls=%async_computation.4 | async-start | bytes 4456448 | tf_op jit(solution)/shard_map/reduce_scatter | solution.py:53
  74.3 17.7 %collective-permute-start.14 = (bf16[384,128]{1,0:T(8,128)(2,1)S(1)}, bf16[384,128]{1,0:T(8,128)(2,1)S(1)}, u32[]{:S(2)}, u32[]{:S(2)}) collective-permute-start(bf16[384,128]{1,0:T(8,128)(2,1)S(1)} %collective-permute-done.13), channel_id=1, source_target_pairs={{0,240},{16,0},{32,16},{48,32},{64,48},{80,64},{96,80},{112,96},{1... | collective-permute-start | bytes 294920 | tf_op jit(solution)/shard_map/ppermute | solution.py:20
  219.3 215.3 %copy-start.8 = (f32[2048]{0:T(1024)S(1)}, f32[2048]{0:T(1024)}, u32[]{:S(2)}) copy-start(f32[2048]{0:T(1024)} %param.15) | copy-start | bytes 24580
  219.4 149.5 %all-gather.12.cloned.1.call-start = ((), (), s32[]{:S(2)}) async-start(), calls=%async_computation.5 | async-start | bytes 2228224 | tf_op jit(solution)/shard_map/all_gather | solution.py:55
  291.8 142.9 %all-gather.14.cloned.1.call-start = ((), (), s32[]{:S(2)}) async-start(), calls=%async_computation.6 | async-start | bytes 1114112 | tf_op jit(solution)/shard_map/all_gather | solution.py:61
  292.6 149.1 %collective-permute-start.15 = (bf16[512,128]{1,0:T(8,128)(2,1)}, bf16[512,128]{1,0:T(8,128)(2,1)S(1)}, u32[]{:S(2)}, u32[]{:S(2)}) collective-permute-start(bf16[512,128]{1,0:T(8,128)(2,1)} %add_convert_fusion), channel_id=1, source_target_pairs={{0,256},{256,0},{1,257},{257,1},{2,258},{258,2},{3,259},{259,3},{4... | collective-permute-start | bytes 393224 | tf_op jit(solution)/shard_map/ppermute | solution.py:26
  437.6 6.2 %collective-permute-start.16 = (bf16[512,256]{0,1:T(8,128)(2,1)S(1)}, bf16[512,256]{0,1:T(8,128)(2,1)S(1)}, u32[]{:S(2)}, u32[]{:S(2)}) collective-permute-start(bf16[512,256]{0,1:T(8,128)(2,1)S(1)} %fusion.24), channel_id=1, source_target_pairs={{0,256},{256,0},{1,257},{257,1},{2,258},{258,2},{3,259},{259,3},{4... | collective-permute-start | bytes 786440 | tf_op jit(solution)/shard_map/ppermute | solution.py:26
  (8 other events, 621.4 us)
Sparse Core Ops, SparseCore 0:
  10.0 74.3 all-gather.5
  87.4 63.8 all-gather.7
  154.3 58.7 all-gather.9
  219.5 70.5 reduce-scatter.1
  292.5 76.3 all-gather.11
  371.8 62.8 all-gather.13
